TPU v7x, 256 devices: a whole 4x4x8 slice. The times are simulated.
256 devices in a mesh: dp: 8 (over y, z_lo), fsdp: 32 (over z_hi, x, core).
Axes of the slice: x: 4, y: 4, z: 8 (z_hi: 4, z_lo: 2; z = z_hi * 2 + z_lo), core: 2. Of those that a mesh axis runs over, the one named last changes fastest.
Arguments:
- acts: bfloat16 [114688, 7168], P(('dp', 'fsdp')), may hold values from -24 to 24
- upstream: bfloat16 [114688, 512], P(('dp', 'fsdp')), may hold values from -0.4375 to 0.4375
- k_weight: bfloat16 [7168, 512], P('fsdp'), may hold values from -0.0625 to 0.0625
- probe: bfloat16 [7168, 512], P('fsdp'), may hold values from -5 to 5
- norm_gain: float32 [128], replicated, may hold values from 0.1 to 1.9
- momentum: float32 [7168, 512], P('fsdp', 'dp'), may hold values from -4 to 4
- curvature: float32 [7168, 512], P('fsdp', 'dp'), may hold values from 0.3 to 3
Outputs:
- new_momentum: float32 [7168, 512], P('fsdp', 'dp')
- new_curvature: float32 [7168, 512], P('fsdp', 'dp')
- update: float32 [7168, 512], P('fsdp', 'dp')
All inputs are finite; a program needn't handle non-finite values.
Results may differ from a plain program's by a relative error of at most 0.024.
Values may be sent and summed in bfloat16 or wider, within the bound.
A program may use at most 128 MiB of HBM per device.

v0:
```python
import jax
import jax.numpy as jnp
from jax import lax
from jax.sharding import PartitionSpec as P


def head_terms(projected, tangent, upstream, norm_gain):
    token_count = projected.shape[0]
    head_size = norm_gain.shape[0]
    head_count = projected.shape[1] // head_size
    shaped = (token_count, head_count, head_size)
    values = projected.reshape(shaped)
    moving = tangent.reshape(shaped)
    weighted = upstream.astype(jnp.float32).reshape(shaped) * norm_gain
    inverse = lax.rsqrt(jnp.mean(values * values, axis=-1, keepdims=True) + 1e-06)
    cubed = inverse * inverse * inverse
    along = jnp.sum(weighted * values, axis=-1, keepdims=True)
    grad_vals = inverse * weighted - cubed * values * along / head_size
    inverse_dot = -cubed * jnp.sum(values * moving, axis=-1, keepdims=True) / head_size
    along_dot = jnp.sum(weighted * moving, axis=-1, keepdims=True)
    hvp_vals = (
        inverse_dot * weighted
        - (
            3.0 * inverse * inverse * inverse_dot * values * along
            + cubed * moving * along
            + cubed * values * along_dot
        )
        / head_size
    )
    return (grad_vals.reshape(token_count, -1), hvp_vals.reshape(token_count, -1))


def contract_tokens(left, right):
    return lax.dot_general(
        left, right, (((0,), (0,)), ((), ())), preferred_element_type=jnp.float32
    )


def on_device(acts, upstream, k_weight, probe, norm_gain, momentum, curvature):
    width = k_weight.shape[1]
    weight_piece = lax.all_gather(k_weight, "fsdp", axis=0, tiled=True)
    probe_piece = lax.all_gather(probe, "fsdp", axis=0, tiled=True)
    projected = jnp.dot(acts, weight_piece, preferred_element_type=jnp.float32)
    tangent = jnp.dot(acts, probe_piece, preferred_element_type=jnp.float32)
    grad_vals, hvp_vals = head_terms(projected, tangent, upstream, norm_gain)
    stacked = jnp.concatenate([grad_vals, hvp_vals], axis=1).astype(jnp.bfloat16)
    owned = lax.psum_scatter(
        contract_tokens(acts, stacked).astype(jnp.bfloat16), "fsdp", scatter_dimension=0, tiled=True
    ).astype(jnp.float32)
    grad_owned = owned[:, :width]
    hvp_owned = owned[:, width:]
    grad_share, hvp_share = (
        lax.psum_scatter(grad_owned, "dp", scatter_dimension=1, tiled=True),
        lax.psum_scatter(hvp_owned, "dp", scatter_dimension=1, tiled=True),
    )
    share_width = grad_share.shape[1]
    probe_cols = lax.dynamic_slice_in_dim(
        probe, lax.axis_index("dp") * share_width, share_width, 1
    ).astype(jnp.float32)
    new_momentum = 0.965 * momentum + 0.035 * grad_share
    new_curvature = 0.99 * curvature + 0.01 * (probe_cols * hvp_share)
    update = jnp.clip(new_momentum / jnp.maximum(0.5 * new_curvature, 0.25), -1.0, 1.0)
    return (new_momentum, new_curvature, update)


def solution(mesh):
    return jax.shard_map(
        on_device,
        mesh=mesh,
        in_specs=(
            P(("dp", "fsdp"), None),
            P(("dp", "fsdp"), None),
            P("fsdp", None),
            P("fsdp", None),
            P(),
            P("fsdp", "dp"),
            P("fsdp", "dp"),
        ),
        out_specs=(P("fsdp", "dp"), P("fsdp", "dp"), P("fsdp", "dp")),
        check_vma=False,
    )
```

profile of v0, /device:TPU:2, one launch (start us, length us, event | category | flops | bytes accessed | tf_op | source)
XLA Modules:
  0.0 465.9 jit_solution(4802881140647189085)
XLA Ops:
  7.2 0.0 all-gather.3.cloned.1.call-start
  7.2 0.7 all-gather.3.cloned.1.call-update
  7.9 0.0 all-gather.5.cloned.1.call-start
  7.9 0.7 all-gather.5.cloned.1.call-update
  8.6 0.0 reduce-scatter.10.cloned.1.call-start
  8.7 1.3 reshape.67
  10.0 0.7 broadcast_bitcast_fusion
  10.7 75.3 %all-gather.3.cloned.1.call-done = bf16[7168,512]{1,0:T(8,128)(2,1)} async-done(((bf16[224,512]{1,0:T(8,128)(2,1)}), bf16[7168,512]{1,0:T(8,128)(2,1)}) %all-gather.3.cloned.1.call-update) | async-done | bytes 7340048 | tf_op jit(solution)/shard_map/all_gather | solution.py:41
  86.0 7.7 %fusion.23 = f32[448,512]{1,0:T(8,128)S(1)} fusion(bf16[448,7168]{1,0:T(8,128)(2,1)} %param.7, bf16[7168,512]{1,0:T(8,128)(2,1)} %all-gather.3.cloned.1.call-done), kind=kOutput, calls=%fused_computation.44 | convolution fusion | flops 3288334336 | bytes 14680064 | tf_op jit(solution)/shard_map/dot_general | solution.py:43
  93.7 0.0 copy-start
  93.7 0.3 reshape.66
  94.0 0.0 copy-start.7
  94.0 66.8 %all-gather.5.cloned.1.call-done = bf16[7168,512]{1,0:T(8,128)(2,1)} async-done(((bf16[224,512]{1,0:T(8,128)(2,1)}), bf16[7168,512]{1,0:T(8,128)(2,1)}) %all-gather.5.cloned.1.call-update) | async-done | bytes 7340048 | tf_op jit(solution)/shard_map/all_gather | solution.py:42
  160.8 0.0 copy-done
  160.8 9.4 %fusion.24 = f32[448,512]{1,0:T(8,128)} fusion(bf16[448,7168]{1,0:T(8,128)(2,1)} %param.7, bf16[7168,512]{1,0:T(8,128)(2,1)} %all-gather.5.cloned.1.call-done), kind=kOutput, calls=%fused_computation.45 | convolution fusion | flops 3288334336 | bytes 14680064 | tf_op jit(solution)/shard_map/dot_general | solution.py:44
  170.2 1.5 reshape.68
  171.7 0.0 copy-start.4
  171.7 1.6 multiply_reduce_fusion.3
  173.3 0.0 copy-done.7
  173.3 1.5 fusion
  174.9 0.0 copy-start.1
  174.9 1.5 fusion.1
  176.3 0.0 copy-start.2
  176.3 0.0 copy-start.3
  176.3 1.2 copy.17
  177.5 0.1 copy.20
  177.7 0.1 copy.22
  177.8 0.9 copy.18
  178.7 0.8 copy.19
  179.5 0.8 copy.21
  180.3 0.0 slice-start
  180.3 0.5 mul.254
  180.9 1.7 mul.227
  182.6 1.5 mul.236
  184.1 1.5 mul.247
  185.6 0.0 copy-done.4
  185.6 0.0 copy-done.1
  185.6 0.0 copy-done.2
  185.6 0.0 copy-done.3
  185.6 0.0 slice-start.1
  185.6 2.3 fusion.10
  187.9 0.0 slice-done
  187.9 0.0 slice-done.1
  188.0 11.3 %convert_bitcast_fusion = bf16[7168,1024]{0,1:T(8,128)(2,1)} fusion(bf16[448,7168]{1,0:T(8,128)(2,1)S(1)} %bitcast.67, bf16[448,512]{1,0:T(8,128)(2,1)S(1)} %get-tuple-element.9, bf16[448,512]{1,0:T(8,128)(2,1)S(1)} %get-tuple-element.8), kind=kOutput, calls=%fused_computation.2 | convolution fusion | flops 6585843712 | bytes 22020096 | tf_op jit(solution)/shard_map/dot_general | solution.py:34
  199.3 19.9 %copy.24 = bf16[7168,1024]{1,0:T(8,128)(2,1)} copy(bf16[7168,1024]{0,1:T(8,128)(2,1)} %convert_bitcast_fusion) | data formatting | bytes 29360128
  219.2 0.0 copy-start.5
  219.2 0.0 copy-start.6
  219.2 0.0 reduce-scatter.10.cloned.1.call-update
  219.2 0.0 reduce-scatter.6.cloned.1.call-start
  219.3 154.1 %reduce-scatter.10.cloned.1.call-done = bf16[224,1024]{1,0:T(8,128)(2,1)} async-done(((bf16[7168,1024]{1,0:T(8,128)(2,1)}), bf16[224,1024]{1,0:T(8,128)(2,1)}) %reduce-scatter.10.cloned.1.call-update) | async-done | bytes 458768
  373.3 1.2 copy.25
  374.6 1.0 fusion.22
  375.6 0.0 reduce-scatter.6.cloned.1.call-update
  375.6 0.0 reduce-scatter.8.cloned.1.call-start
  375.7 0.5 reduce-scatter.8.cloned.1.call-update
  376.2 0.9 constant_dynamic-slice_fusion
  377.1 0.1 copy.26
  377.2 38.8 %reduce-scatter.6.cloned.1.call-done = f32[224,64]{0,1:T(8,128)} async-done(((f32[224,512]{0,1:T(8,128)}), f32[224,64]{0,1:T(8,128)}) %reduce-scatter.6.cloned.1.call-update) | async-done | bytes 57360 | tf_op jit(solution)/shard_map/reduce_scatter | solution.py:53
  416.0 41.8 %reduce-scatter.8.cloned.1.call-done = f32[224,64]{0,1:T(8,128)} async-done(((f32[224,512]{0,1:T(8,128)}), f32[224,64]{0,1:T(8,128)}) %reduce-scatter.8.cloned.1.call-update) | async-done | bytes 57360 | tf_op jit(solution)/shard_map/reduce_scatter | solution.py:54
  457.8 0.0 copy-done.5
  457.8 0.0 copy-done.6
  457.8 1.6 divide_clamp_fusion
  (2 shorter events, 0.0 us)
Async XLA Ops:
  7.2 78.8 %all-gather.3.cloned.1.call-start = ((), (), s32[]{:S(2)}) async-start(), calls=%async_computation.3 | async-start | bytes 7569408 | tf_op jit(solution)/shard_map/all_gather | solution.py:41
  7.9 152.9 %all-gather.5.cloned.1.call-start = ((), (), s32[]{:S(2)}) async-start(), calls=%async_computation.4 | async-start | bytes 7569408 | tf_op jit(solution)/shard_map/all_gather | solution.py:42
  8.6 364.7 %reduce-scatter.10.cloned.1.call-start = ((), (), s32[]{:S(2)}) async-start(), calls=%async_computation.7 | async-start | bytes 15138816
  93.7 67.1 %copy-start = (f32[448,512]{1,0:T(8,128)}, f32[448,512]{1,0:T(8,128)S(1)}, u32[]{:S(2)}) copy-start(f32[448,512]{1,0:T(8,128)S(1)} %fusion.23) | copy-start | bytes 2752516
  94.0 79.3 %copy-start.7 = (f32[128]{0:T(128)S(1)}, f32[128]{0:T(128)}, u32[]{:S(2)}) copy-start(f32[128]{0:T(128)} %param.11) | copy-start | bytes 1540
  171.7 13.9 %copy-start.4 = (bf16[448,512]{1,0:T(8,128)(2,1)S(1)}, bf16[448,512]{1,0:T(8,128)(2,1)}, u32[]{:S(2)}) copy-start(bf16[448,512]{1,0:T(8,128)(2,1)} %param.8) | copy-start | bytes 1376260
  174.9 10.7 %copy-start.1 = (f32[448,512]{1,0:T(8,128)S(1)}, f32[448,512]{1,0:T(8,128)}, u32[]{:S(2)}) copy-start(f32[448,512]{1,0:T(8,128)} %copy-done) | copy-start | bytes 2752516
  176.3 9.3 %copy-start.2 = (f32[448,512]{1,0:T(8,128)S(1)}, f32[448,512]{1,0:T(8,128)}, u32[]{:S(2)}) copy-start(f32[448,512]{1,0:T(8,128)} %fusion.24) | copy-start | bytes 2752516
  176.3 9.3 %copy-start.3 = (f32[448,4,128]{2,1,0:T(4,128)S(1)}, f32[448,4,128]{2,1,0:T(4,128)}, u32[]{:S(2)}) copy-start(f32[448,4,128]{2,1,0:T(4,128)} %fusion) | copy-start | bytes 2752516
  180.3 7.6 %slice-start = ((s8[6422528]{0:T(1024)(128)(4,1)}), s8[4194304]{0:T(1024)(128)(4,1)S(1)}, s32[]{:S(2)}) async-start(s8[6422528]{0:T(1024)(128)(4,1)} %bitcast.66), calls=%async_computation.8 | async-start | bytes 8388608
  185.6 2.3 slice-start.1
  219.2 238.6 %copy-start.5 = (f32[224,64]{0,1:T(8,128)S(1)}, f32[224,64]{0,1:T(8,128)}, u32[]{:S(2)}) copy-start(f32[224,64]{0,1:T(8,128)} %param.13) | copy-start | bytes 172036
  219.2 238.6 %copy-start.6 = (f32[224,64]{0,1:T(8,128)S(1)}, f32[224,64]{0,1:T(8,128)}, u32[]{:S(2)}) copy-start(f32[224,64]{0,1:T(8,128)} %param.12) | copy-start | bytes 172036
  219.2 196.8 %reduce-scatter.6.cloned.1.call-start = ((), (), s32[]{:S(2)}) async-start(), calls=%async_computation.5 | async-start | bytes 589824 | tf_op jit(solution)/shard_map/reduce_scatter | solution.py:53
  375.6 82.2 %reduce-scatter.8.cloned.1.call-start = ((), (), s32[]{:S(2)}) async-start(), calls=%async_computation.6 | async-start | bytes 589824 | tf_op jit(solution)/shard_map/reduce_scatter | solution.py:54
Sparse Core Ops, SparseCore 0:
  10.5 75.4 all-gather.2
  88.5 72.2 all-gather.4
  219.3 153.9 reduce-scatter.9
  375.8 40.2 reduce-scatter.5
  418.4 39.4 reduce-scatter.7
where the time goes:
time: 467 us; the launch traced here: 466 us
  waiting for transfers between devices  379 us (81%)
  local copies, waits for them, and re-layouts  36.1 us (8%)
  matrix products  28.4 us (6%)
  between operations  13.9 us (3%)
  other arithmetic  8.53 us (2%)
    unnamed x6, waiting for transfers between devices  156 us
    all_gather x1, waiting for transfers between devices, on_device(): weight_piece = lax.all_gather(k_weight, 'fsdp', axis=0, tiled=True)  75.3 us
    all_gather x1, waiting for transfers between devices, on_device(): probe_piece = lax.all_gather(probe, 'fsdp', axis=0, tiled=True)  66.8 us
    reduce_scatter x1, waiting for transfers between devices, on_device(): lax.psum_scatter(hvp_owned, 'dp', scatter_dimension=1, tiled=True)  41.8 us
    reduce_scatter x1, waiting for transfers between devices, on_device(): lax.psum_scatter(grad_owned, 'dp', scatter_dimension=1, tiled=True)  38.8 us
    unnamed x23, local copies, waits for them, and re-layouts  21.3 us
    dot_general x1, matrix products, contract_tokens(): lax.dot_general(left, right, (((0,), (0,)), ((), ())), preferred_element_...  11.3 us
    dot_general x1, matrix products, on_device(): tangent = jnp.dot(acts, probe_piece, preferred_element_type=jnp.float32)  9.36 us
  transfers between devices with their start and end apart: 5, of which 5 were waited for; matrix products, arithmetic and copies ran while one was open for 2% of the time, Pallas kernels for 0%

commit v1 on v0

--- a/solution.py
+++ b/solution.py
@@ -38,7 +38,9 @@
 
 def on_device(acts, upstream, k_weight, probe, norm_gain, momentum, curvature):
     width = k_weight.shape[1]
-    weight_piece = lax.all_gather(k_weight, "fsdp", axis=0, tiled=True)
+    weight_piece = jnp.concatenate(
+        lax.all_to_all(jnp.stack([k_weight] * lax.axis_size("fsdp")), "fsdp", 0, 0), axis=0
+    )
     probe_piece = lax.all_gather(probe, "fsdp", axis=0, tiled=True)
     projected = jnp.dot(acts, weight_piece, preferred_element_type=jnp.float32)
     tangent = jnp.dot(acts, probe_piece, preferred_element_type=jnp.float32)

time: 467 us -> 529 us (1.13)
  waiting for transfers between devices: 379 us -> 432 us
  starting transfers between devices: 0.2 us -> 11.8 us
    all_to_all x0 -> x1, waiting for transfers between devices: none -> 199 us  [on_device(): lax.all_to_all(jnp.stack([k_weight] * lax.axis_size('fsdp')), 'fsdp', 0, 0)]
    all_gather x1 -> x0, waiting for transfers between devices: 75.3 us -> none  [on_device(): weight_piece = lax.all_gather(k_weight, 'fsdp', axis=0, tiled=True)]
    all_gather x1, waiting for transfers between devices: 66.8 us -> 0.01 us  [on_device(): probe_piece = lax.all_gather(probe, 'fsdp', axis=0, tiled=True)]
    all_to_all x0 -> x1, starting transfers between devices: none -> 11.7 us  [on_device(): lax.all_to_all(jnp.stack([k_weight] * lax.axis_size('fsdp')), 'fsdp', 0, 0)]
    dot_general x0 -> x1, local copies, waits for them, and re-layouts: none -> 9.98 us  [on_device(): projected = jnp.dot(acts, weight_piece, preferred_element_type=jnp.float32)]
    mul x7 -> x0, local copies, waits for them, and re-layouts: 6.84 us -> none  [the longest x2 3.21 us: head_terms(): grad_vals = inverse * weighted - cubed * values * along / head_size]
    unnamed x6 -> x5, waiting for transfers between devices: 156 us -> 152 us
    unnamed x23 -> x17, local copies, waits for them, and re-layouts: 21.3 us -> 21.2 us
  transfers between devices with their start and end apart: 5 -> 5, of which waited for: 5 -> 4; matrix products, arithmetic and copies ran while one was open for 2% -> 2% of each run, Pallas kernels for 0% -> 0%
where the time goes in v1:
time: 529 us; the launch traced here: 528 us
  waiting for transfers between devices  432 us (82%)
  local copies, waits for them, and re-layouts  37.9 us (7%)
  matrix products  26.2 us (5%)
  between operations  13.9 us (3%)
  starting transfers between devices  11.8 us (2%)
  other arithmetic  5.9 us (1%)
    all_to_all x1, waiting for transfers between devices, on_device(): lax.all_to_all(jnp.stack([k_weight] * lax.axis_size('fsdp')), 'fsdp', 0, 0)  199 us
    unnamed x5, waiting for transfers between devices  152 us
    reduce_scatter x1, waiting for transfers between devices, on_device(): lax.psum_scatter(hvp_owned, 'dp', scatter_dimension=1, tiled=True)  41.7 us
    reduce_scatter x1, waiting for transfers between devices, on_device(): lax.psum_scatter(grad_owned, 'dp', scatter_dimension=1, tiled=True)  39.2 us
    unnamed x17, local copies, waits for them, and re-layouts  21.2 us
    all_to_all x1, starting transfers between devices, on_device(): lax.all_to_all(jnp.stack([k_weight] * lax.axis_size('fsdp')), 'fsdp', 0, 0)  11.7 us
    dot_general x1, matrix products, contract_tokens(): lax.dot_general(left, right, (((0,), (0,)), ((), ())), preferred_element_...  11.1 us
  transfers between devices with their start and end apart: 5, of which 4 were waited for; matrix products, arithmetic and copies ran while one was open for 2% of the time, Pallas kernels for 0%

profile of v1, /device:TPU:2, one launch (start us, length us, event | category | flops | bytes accessed | tf_op | source)
XLA Modules:
  0.0 528.1 jit_solution(8030077217894572399)
XLA Ops:
  7.2 4.7 stack.2
  11.9 11.7 %all-to-all-start = ((bf16[32,224,512]{2,1,0:T(8,128)(2,1)}), bf16[32,224,512]{2,1,0:T(8,128)(2,1)}, u32[]{:S(2)}, u32[]{:S(2)}) async-start(bf16[32,224,512]{2,1,0:T(8,128)(2,1)} %stack.2), calls=%async_computation | async-start | bytes 14680064 | tf_op jit(solution)/shard_map/all_to_all | solution.py:42
  23.5 0.0 all-gather.2.cloned.1.call-start
  23.6 0.7 all-gather.2.cloned.1.call-update
  24.3 0.0 reduce-scatter.10.cloned.1.call-start
  24.3 199.5 %all-to-all-done = bf16[32,224,512]{2,1,0:T(8,128)(2,1)} async-done(((bf16[32,224,512]{2,1,0:T(8,128)(2,1)}), bf16[32,224,512]{2,1,0:T(8,128)(2,1)}, u32[]{:S(2)}, u32[]{:S(2)}) %all-to-all-start) | async-done | bytes 7340064 | tf_op jit(solution)/shard_map/all_to_all | solution.py:42
  223.8 10.0 %copy.20 = bf16[512,7168]{1,0:T(8,128)(2,1)} copy(bf16[512,7168]{0,1:T(8,128)(2,1)} %bitcast.2) | data formatting | bytes 14680064 | tf_op jit(solution)/shard_map/dot_general | solution.py:45
  233.8 0.0 copy-start.1
  233.8 0.0 copy-start.4
  233.8 0.0 all-gather.2.cloned.1.call-done
  233.8 0.0 copy-start
  233.8 0.0 slice-start
  233.8 7.8 %convolution_bitcast_fusion = f32[56,4,8,128]{3,2,1,0:T(8,128)S(1)} fusion(bf16[448,7168]{1,0:T(8,128)(2,1)} %param.7, bf16[7168,512]{1,0:T(8,128)(2,1)} %all-gather.2.cloned.1.call-done), kind=kOutput, calls=%fused_computation.8 | convolution fusion | flops 3288334336 | bytes 14680064 | tf_op jit(solution)/shard_map/dot_general | solution.py:46
  241.6 0.0 copy-done.1
  241.6 0.0 copy-done.4
  241.7 0.0 copy-done
  241.7 0.0 slice-start.1
  241.7 7.3 %multiply_reduce_fusion = (f32[448,4]{0,1:T(4,128)S(1)}, f32[448,4]{0,1:T(4,128)S(1)}, f32[448,4]{0,1:T(4,128)S(1)}, f32[448,4,128]{2,0,1:T(8,128)S(1)}) fusion(f32[128]{0:T(128)S(1)} %copy-done.4, f32[56,4,8,128]{3,2,1,0:T(8,128)S(1)} %convolution_bitcast_fusion, bf16[4,128,7168]{2,1,0:T(8,128)(2,1)S(1)} %bitcast.66, bf16[448,7168]{1,0:T(8,128)(2,1)} %param.7, ...), kind=kOutput, calls=%fused_computation.23 | convolution fusion | flops 3290163968 | bytes 16078336 | tf_op jit(solution)/shard_map/dot_general | solution.py:45
  249.0 3.3 fusion.8
  252.3 1.0 copy_bitcast_fusion
  253.3 0.0 slice-done
  253.3 0.0 slice-done.1
  253.4 11.1 %convert_bitcast_fusion = bf16[7168,1024]{0,1:T(8,128)(2,1)} fusion(bf16[448,7168]{1,0:T(8,128)(2,1)S(1)} %bitcast.68, bf16[448,512]{1,0:T(8,128)(2,1)S(1)} %get-tuple-element.18, bf16[448,512]{1,0:T(8,128)(2,1)S(1)} %get-tuple-element.19), kind=kOutput, calls=%fused_computation.1 | convolution fusion | flops 6585843712 | bytes 22020096 | tf_op jit(solution)/shard_map/dot_general | solution.py:34
  264.4 19.9 %copy.28 = bf16[7168,1024]{1,0:T(8,128)(2,1)} copy(bf16[7168,1024]{0,1:T(8,128)(2,1)} %convert_bitcast_fusion) | data formatting | bytes 29360128
  284.3 0.0 copy-start.2
  284.3 0.0 copy-start.3
  284.3 0.0 reduce-scatter.10.cloned.1.call-update
  284.4 0.0 reduce-scatter.6.cloned.1.call-start
  284.4 150.8 %reduce-scatter.10.cloned.1.call-done = bf16[224,1024]{1,0:T(8,128)(2,1)} async-done(((bf16[7168,1024]{1,0:T(8,128)(2,1)}), bf16[224,1024]{1,0:T(8,128)(2,1)}) %reduce-scatter.10.cloned.1.call-update) | async-done | bytes 458768
  435.2 1.2 copy.29
  436.5 1.0 fusion.20
  437.5 0.0 reduce-scatter.6.cloned.1.call-update
  437.5 0.0 reduce-scatter.8.cloned.1.call-start
  437.6 0.5 reduce-scatter.8.cloned.1.call-update
  438.1 0.9 constant_dynamic-slice_fusion
  439.0 0.1 copy.30
  439.1 39.2 %reduce-scatter.6.cloned.1.call-done = f32[224,64]{0,1:T(8,128)} async-done(((f32[224,512]{0,1:T(8,128)}), f32[224,64]{0,1:T(8,128)}) %reduce-scatter.6.cloned.1.call-update) | async-done | bytes 57360 | tf_op jit(solution)/shard_map/reduce_scatter | solution.py:55
  478.3 41.7 %reduce-scatter.8.cloned.1.call-done = f32[224,64]{0,1:T(8,128)} async-done(((f32[224,512]{0,1:T(8,128)}), f32[224,64]{0,1:T(8,128)}) %reduce-scatter.8.cloned.1.call-update) | async-done | bytes 57360 | tf_op jit(solution)/shard_map/reduce_scatter | solution.py:56
  520.0 0.0 copy-done.2
  520.0 0.0 copy-done.3
  520.0 1.6 divide_clamp_fusion
  (2 shorter events, 0.0 us)
Async XLA Ops:
  11.9 211.9 %all-to-all-start = ((bf16[32,224,512]{2,1,0:T(8,128)(2,1)}), bf16[32,224,512]{2,1,0:T(8,128)(2,1)}, u32[]{:S(2)}, u32[]{:S(2)}) async-start(bf16[32,224,512]{2,1,0:T(8,128)(2,1)} %stack.2), calls=%async_computation | async-start | bytes 14680064 | tf_op jit(solution)/shard_map/all_to_all | solution.py:42
  23.5 210.2 %all-gather.2.cloned.1.call-start = ((), (), s32[]{:S(2)}) async-start(), calls=%async_computation.4 | async-start | bytes 7569408 | tf_op jit(solution)/shard_map/all_gather | solution.py:44
  24.3 411.0 %reduce-scatter.10.cloned.1.call-start = ((), (), s32[]{:S(2)}) async-start(), calls=%async_computation.7 | async-start | bytes 15138816
  233.8 7.9 %copy-start.1 = (bf16[448,512]{1,0:T(8,128)(2,1)S(1)}, bf16[448,512]{1,0:T(8,128)(2,1)}, u32[]{:S(2)}) copy-start(bf16[448,512]{1,0:T(8,128)(2,1)} %param.8) | copy-start | bytes 1376260
  233.8 7.9 %copy-start.4 = (f32[128]{0:T(128)S(1)}, f32[128]{0:T(128)}, u32[]{:S(2)}) copy-start(f32[128]{0:T(128)} %param.11) | copy-start | bytes 1540
  233.8 7.9 %copy-start = (bf16[512,7168]{1,0:T(8,128)(2,1)S(1)}, bf16[512,7168]{1,0:T(8,128)(2,1)}, u32[]{:S(2)}) copy-start(bf16[512,7168]{1,0:T(8,128)(2,1)} %copy.20) | copy-start | bytes 22020100
  233.8 19.5 %slice-start = ((s8[6422528]{0:T(1024)(128)(4,1)}), s8[4194304]{0:T(1024)(128)(4,1)S(1)}, s32[]{:S(2)}) async-start(s8[6422528]{0:T(1024)(128)(4,1)} %bitcast.67), calls=%async_computation.8 | async-start | bytes 8388608
  241.7 11.7 %slice-start.1 = ((s8[6422528]{0:T(1024)(128)(4,1)}), s8[2228224]{0:T(1024)(128)(4,1)S(1)}, s32[]{:S(2)}) async-start(s8[6422528]{0:T(1024)(128)(4,1)} %bitcast.67), calls=%async_computation.9 | async-start | bytes 4456448
  284.3 235.7 %copy-start.2 = (f32[224,64]{0,1:T(8,128)S(1)}, f32[224,64]{0,1:T(8,128)}, u32[]{:S(2)}) copy-start(f32[224,64]{0,1:T(8,128)} %param.13) | copy-start | bytes 172036
  284.3 235.7 %copy-start.3 = (f32[224,64]{0,1:T(8,128)S(1)}, f32[224,64]{0,1:T(8,128)}, u32[]{:S(2)}) copy-start(f32[224,64]{0,1:T(8,128)} %param.12) | copy-start | bytes 172036
  284.4 193.9 %reduce-scatter.6.cloned.1.call-start = ((), (), s32[]{:S(2)}) async-start(), calls=%async_computation.5 | async-start | bytes 589824 | tf_op jit(solution)/shard_map/reduce_scatter | solution.py:55
  437.5 82.5 %reduce-scatter.8.cloned.1.call-start = ((), (), s32[]{:S(2)}) async-start(), calls=%async_computation.6 | async-start | bytes 589824 | tf_op jit(solution)/shard_map/reduce_scatter | solution.py:56
Sparse Core Ops, SparseCore 0:
  26.9 181.2 all-gather.1
  284.5 150.6 reduce-scatter.9
  437.8 40.4 reduce-scatter.5
  480.6 39.3 reduce-scatter.7
